TPU v7x, 256 devices: a whole 4x4x8 slice. The times are simulated.
256 devices in a mesh: gx: 8 (over y, core), gy: 4 (over z_lo), gz: 8 (over z_hi, x).
Axes of the slice: x: 4, y: 4, z: 8 (z_hi: 2, z_lo: 4; z = z_hi * 4 + z_lo), core: 2. Of those that a mesh axis runs over, the one named last changes fastest.
Arguments:
- tokens: bfloat16 [2048, 8192], P(('gx', 'gy'), 'gz'), may hold values from -6 to 6
- gate_weight: bfloat16 [8192, 28672], P('gz', ('gx', 'gy')), may hold values from -0.0625 to 0.0625
- up_weight: bfloat16 [8192, 28672], P('gz', ('gx', 'gy')), may hold values from -0.0625 to 0.0625
- down_weight: bfloat16 [28672, 8192], P(('gx', 'gy'), 'gz'), may hold values from -0.03125 to 0.03125
Outputs:
- layer_output: bfloat16 [2048, 8192], P(('gx', 'gy'), 'gz')
All inputs are finite; a program needn't handle non-finite values.
Results may differ from a plain program's by a relative error of at most 0.029.
Values may be sent and summed in bfloat16 or wider, within the bound.
A program may use at most 128 MiB of HBM per device.

v0:
```python
import jax
import jax.numpy as jnp
from jax import lax
from jax.sharding import PartitionSpec as P


def shards(tokens, gate_weight, up_weight, down_weight):
    gathered = lax.all_gather(tokens, "gx", axis=0, tiled=True)

    def column_product(weight_piece):
        return jnp.dot(gathered, weight_piece, preferred_element_type=jnp.float32)

    gate_partial = column_product(lax.all_gather(gate_weight, "gy", axis=1, tiled=True))
    up_partial = column_product(lax.all_gather(up_weight, "gy", axis=1, tiled=True))
    gate_sum, up_sum = (
        lax.psum_scatter(
            gate_partial.astype(jnp.bfloat16), "gz", scatter_dimension=0, tiled=True
        ).astype(jnp.float32),
        lax.psum_scatter(
            up_partial.astype(jnp.bfloat16), "gz", scatter_dimension=0, tiled=True
        ).astype(jnp.float32),
    )
    local_hidden = (jax.nn.silu(gate_sum) * up_sum).astype(jnp.bfloat16)
    hidden = lax.all_gather(local_hidden, "gz", axis=0, tiled=True)
    down_partial = jnp.dot(
        hidden,
        lax.all_gather(down_weight, "gy", axis=0, tiled=True),
        preferred_element_type=jnp.float32,
    )
    layer_output = lax.psum_scatter(
        down_partial.astype(jnp.bfloat16), "gx", scatter_dimension=0, tiled=True
    )
    return layer_output


def solution(mesh):
    return jax.shard_map(
        shards,
        mesh=mesh,
        in_specs=(
            P(("gx", "gy"), "gz"),
            P("gz", ("gx", "gy")),
            P("gz", ("gx", "gy")),
            P(("gx", "gy"), "gz"),
        ),
        out_specs=P(("gx", "gy"), "gz"),
        check_vma=False,
    )
```

profile of v0, /device:TPU:2, one launch (start us, length us, event | category | flops | bytes accessed | tf_op | source)
XLA Modules:
  0.0 839.3 jit_solution(120754620333667691)
XLA Ops:
  6.5 0.7 all-gather.6.cloned.1.call-update
  7.3 0.0 all-gather.8.cloned.1.call-start
  7.3 0.7 all-gather.8.cloned.1.call-update
  8.0 0.0 all-gather.10.cloned.1.call-start
  8.1 0.7 all-gather.10.cloned.1.call-update
  8.7 0.0 reduce-scatter.4.cloned.1.call-start
  8.8 29.3 %all-gather.6.cloned.1.call-done = bf16[512,1024]{1,0:T(8,128)(2,1)} async-done(((bf16[64,1024]{1,0:T(8,128)(2,1)}), bf16[512,1024]{1,0:T(8,128)(2,1)}) %all-gather.6.cloned.1.call-update) | async-done | bytes 1048592 | tf_op jit(solution)/shard_map/all_gather | solution.py:8
  38.1 137.6 %all-gather.8.cloned.1.call-done = bf16[1024,3584]{1,0:T(8,128)(2,1)} async-done(((bf16[1024,896]{1,0:T(8,128)(2,1)}), bf16[1024,3584]{1,0:T(8,128)(2,1)}) %all-gather.8.cloned.1.call-update) | async-done | bytes 7340048 | tf_op jit(solution)/shard_map/all_gather | solution.py:13
  175.7 9.2 %convolution_convert_fusion.1 = bf16[512,3584]{1,0:T(8,128)(2,1)} fusion(bf16[512,1024]{1,0:T(8,128)(2,1)} %all-gather.6.cloned.1.call-done, bf16[1024,3584]{1,0:T(8,128)(2,1)} %all-gather.8.cloned.1.call-done), kind=kOutput, calls=%fused_computation.1 | convolution fusion | flops 3759931392 | bytes 12058624 | tf_op jit(solution)/shard_map/dot_general | solution.py:11
  184.9 0.0 reduce-scatter.6.cloned.1.call-start
  185.0 128.1 %all-gather.10.cloned.1.call-done = bf16[1024,3584]{1,0:T(8,128)(2,1)} async-done(((bf16[1024,896]{1,0:T(8,128)(2,1)}), bf16[1024,3584]{1,0:T(8,128)(2,1)}) %all-gather.10.cloned.1.call-update) | async-done | bytes 7340048 | tf_op jit(solution)/shard_map/all_gather | solution.py:14
  313.1 8.4 %convolution_convert_fusion = bf16[512,3584]{1,0:T(8,128)(2,1)} fusion(bf16[512,1024]{1,0:T(8,128)(2,1)S(1)} %copy-done, bf16[1024,3584]{1,0:T(8,128)(2,1)} %all-gather.10.cloned.1.call-done), kind=kOutput, calls=%fused_computation | convolution fusion | flops 3759931392 | bytes 12058624 | tf_op jit(solution)/shard_map/dot_general | solution.py:11
  321.5 0.0 reduce-scatter.6.cloned.1.call-update
  321.6 0.0 all-gather.14.cloned.1.call-start
  321.6 0.5 all-gather.14.cloned.1.call-update
  322.1 0.0 all-gather.12.cloned.1.call-start
  322.2 115.4 %reduce-scatter.4.cloned.1.call-done = bf16[64,3584]{1,0:T(8,128)(2,1)} async-done(((bf16[512,3584]{1,0:T(8,128)(2,1)}), bf16[64,3584]{1,0:T(8,128)(2,1)}) %reduce-scatter.4.cloned.1.call-update) | async-done | bytes 458768 | tf_op jit(solution)/shard_map/reduce_scatter | solution.py:16
  437.6 121.3 %reduce-scatter.6.cloned.1.call-done = bf16[64,3584]{1,0:T(8,128)(2,1)} async-done(((bf16[512,3584]{1,0:T(8,128)(2,1)}), bf16[64,3584]{1,0:T(8,128)(2,1)}) %reduce-scatter.6.cloned.1.call-update) | async-done | bytes 458768 | tf_op jit(solution)/shard_map/reduce_scatter | solution.py:19
  558.9 2.2 fusion.4
  561.1 0.0 reduce-scatter.8.cloned.1.call-start
  561.2 131.1 %all-gather.14.cloned.1.call-done = bf16[3584,1024]{1,0:T(8,128)(2,1)} async-done(((bf16[896,1024]{1,0:T(8,128)(2,1)}), bf16[3584,1024]{1,0:T(8,128)(2,1)}) %all-gather.14.cloned.1.call-update) | async-done | bytes 7340048 | tf_op jit(solution)/shard_map/all_gather | solution.py:27
  692.3 100.6 %all-gather.12.cloned.1.call-done = bf16[512,3584]{1,0:T(8,128)(2,1)} async-done(((bf16[64,3584]{1,0:T(8,128)(2,1)}), bf16[512,3584]{1,0:T(8,128)(2,1)}) %all-gather.12.cloned.1.call-update) | async-done | bytes 3670032 | tf_op jit(solution)/shard_map/all_gather | solution.py:24
  792.9 9.1 %convolution_convert_fusion.2 = bf16[512,1024]{1,0:T(8,128)(2,1)} fusion(bf16[512,3584]{1,0:T(8,128)(2,1)} %all-gather.12.cloned.1.call-done, bf16[3584,1024]{1,0:T(8,128)(2,1)} %all-gather.14.cloned.1.call-done), kind=kOutput, calls=%fused_computation.2 | convolution fusion | flops 3758620672 | bytes 12058624 | tf_op jit(solution)/shard_map/dot_general | solution.py:25
  802.0 30.5 %reduce-scatter.8.cloned.1.call-done = bf16[64,1024]{1,0:T(8,128)(2,1)} async-done(((bf16[512,1024]{1,0:T(8,128)(2,1)}), bf16[64,1024]{1,0:T(8,128)(2,1)}) %reduce-scatter.8.cloned.1.call-update) | async-done | bytes 131088 | tf_op jit(solution)/shard_map/reduce_scatter | solution.py:30
  (6 shorter events, 0.1 us)
Async XLA Ops:
  6.5 31.6 %all-gather.6.cloned.1.call-start = ((), (), s32[]{:S(2)}) async-start(), calls=%async_computation.3 | async-start | bytes 1179648 | tf_op jit(solution)/shard_map/all_gather | solution.py:8
  7.3 168.4 %all-gather.8.cloned.1.call-start = ((), (), s32[]{:S(2)}) async-start(), calls=%async_computation.4 | async-start | bytes 9175040 | tf_op jit(solution)/shard_map/all_gather | solution.py:13
  8.0 305.1 %all-gather.10.cloned.1.call-start = ((), (), s32[]{:S(2)}) async-start(), calls=%async_computation.6 | async-start | bytes 9175040 | tf_op jit(solution)/shard_map/all_gather | solution.py:14
  8.7 428.9 %reduce-scatter.4.cloned.1.call-start = ((), (), s32[]{:S(2)}) async-start(), calls=%async_computation.5 | async-start | bytes 4128768 | tf_op jit(solution)/shard_map/reduce_scatter | solution.py:16
  38.1 275.0 %copy-start = (bf16[512,1024]{1,0:T(8,128)(2,1)S(1)}, bf16[512,1024]{1,0:T(8,128)(2,1)}, u32[]{:S(2)}) copy-start(bf16[512,1024]{1,0:T(8,128)(2,1)} %all-gather.6.cloned.1.call-done) | copy-start | bytes 3145732
  184.9 374.0 %reduce-scatter.6.cloned.1.call-start = ((), (), s32[]{:S(2)}) async-start(), calls=%async_computation.7 | async-start | bytes 4128768 | tf_op jit(solution)/shard_map/reduce_scatter | solution.py:19
  321.6 370.7 %all-gather.14.cloned.1.call-start = ((), (), s32[]{:S(2)}) async-start(), calls=%async_computation.9 | async-start | bytes 9175040 | tf_op jit(solution)/shard_map/all_gather | solution.py:27
  322.1 470.7 %all-gather.12.cloned.1.call-start = ((), (), s32[]{:S(2)}) async-start(), calls=%async_computation.8 | async-start | bytes 4128768 | tf_op jit(solution)/shard_map/all_gather | solution.py:24
  561.1 271.4 %reduce-scatter.8.cloned.1.call-start = ((), (), s32[]{:S(2)}) async-start(), calls=%async_computation.10 | async-start | bytes 1179648 | tf_op jit(solution)/shard_map/reduce_scatter | solution.py:30
Sparse Core Ops, SparseCore 0:
  9.2 28.8 all-gather.5
  40.0 135.6 all-gather.7
  177.5 135.5 all-gather.9
  317.2 120.3 reduce-scatter.3
  442.3 116.5 reduce-scatter.5
  560.6 131.6 all-gather.13
  694.9 97.9 all-gather.11
  802.1 30.3 reduce-scatter.7
where the time goes:
time: 839 us
  waiting for transfers between devices  797 us (95%)
  matrix products  26.8 us (3%)
  between operations  13.5 us (2%)
    all_gather x1, waiting for transfers between devices, shards(): lax.all_gather(gate_weight, 'gy', axis=1, tiled=True)  138 us
    all_gather x1, waiting for transfers between devices, shards(): lax.all_gather(down_weight, 'gy', axis=0, tiled=True)  131 us
    all_gather x1, waiting for transfers between devices, shards(): lax.all_gather(up_weight, 'gy', axis=1, tiled=True)  128 us
    reduce_scatter x1, waiting for transfers between devices, shards(): lax.psum_scatter(up_partial.astype(jnp.bfloat16), 'gz', scatter_dimension...  121 us
    reduce_scatter x1, waiting for transfers between devices, shards(): lax.psum_scatter(gate_partial.astype(jnp.bfloat16), 'gz', scatter_dimensi...  115 us
    all_gather x1, waiting for transfers between devices, shards(): hidden = lax.all_gather(local_hidden, 'gz', axis=0, tiled=True)  101 us
    reduce_scatter x1, waiting for transfers between devices, shards(): lax.psum_scatter(down_partial.astype(jnp.bfloat16), 'gx', scatter_dimensi...  30.5 us
    all_gather x1, waiting for transfers between devices, shards(): gathered = lax.all_gather(tokens, 'gx', axis=0, tiled=True)  29.3 us
  transfers between devices with their start and end apart: 8, of which 8 were waited for; matrix products, arithmetic and copies ran while one was open for 2% of the time, Pallas kernels for 0%

commit v1 on v0

--- a/solution.py
+++ b/solution.py
@@ -5,7 +5,26 @@
 
 
 def shards(tokens, gate_weight, up_weight, down_weight):
-    gathered = lax.all_gather(tokens, "gx", axis=0, tiled=True)
+    local_next, z_new, small = (lax.axis_size("gx"), lax.axis_index("gx"), tokens.shape[0])
+    items = [ii * local_next if u == 0 else ii for u, ii in enumerate(tokens.shape)]
+    gathered = lax.dynamic_update_slice_in_dim(
+        jnp.zeros(items, tokens.dtype), tokens, z_new * small, axis=0
+    )
+    piece_out = top = tokens
+    for i in range(1, local_next // 2 + 1):
+        piece_out = lax.ppermute(
+            piece_out, axis_name="gx", perm=[(u, (u + 1) % local_next) for u in range(local_next)]
+        )
+        gathered = lax.dynamic_update_slice_in_dim(
+            gathered, piece_out, (z_new - i) % local_next * small, axis=0
+        )
+        if 2 * i < local_next:
+            top = lax.ppermute(
+                top, axis_name="gx", perm=[(u, (u - 1) % local_next) for u in range(local_next)]
+            )
+            gathered = lax.dynamic_update_slice_in_dim(
+                gathered, top, (z_new + i) % local_next * small, axis=0
+            )
 
     def column_product(weight_piece):
         return jnp.dot(gathered, weight_piece, preferred_element_type=jnp.float32)

time: 839 us -> 810 us (0.965)
  waiting for transfers between devices: 797 us -> 758 us
  starting transfers between devices: 0.28 us -> 9.12 us
    all_gather x1 -> x0, waiting for transfers between devices: 29.3 us -> none  [shards(): gathered = lax.all_gather(tokens, 'gx', axis=0, tiled=True)]
    all_gather x1, waiting for transfers between devices: 138 us -> 117 us  [shards(): lax.all_gather(gate_weight, 'gy', axis=1, tiled=True)]
    ppermute x0 -> x7, waiting for transfers between devices: none -> 12.6 us  [the longest x4 12.6 us: shards(): lax.ppermute(piece_out, axis_name='gx', perm=[(u, (u + 1) % local_next) f...]
    ppermute x0 -> x7, starting transfers between devices: none -> 8.88 us  [the longest x3 8.85 us: shards(): lax.ppermute(top, axis_name='gx', perm=[(u, (u - 1) % local_next) for u i...]
  transfers between devices with their start and end apart: 8 -> 14, of which waited for: 8 -> 11; matrix products, arithmetic and copies ran while one was open for 2% -> 3% of each run, Pallas kernels for 0% -> 0%
where the time goes in v1:
time: 810 us
  waiting for transfers between devices  758 us (94%)
  matrix products  26 us (3%)
  between operations  13.6 us (2%)
  starting transfers between devices  9.12 us (1%)
    all_gather x1, waiting for transfers between devices, shards(): lax.all_gather(down_weight, 'gy', axis=0, tiled=True)  131 us
    all_gather x1, waiting for transfers between devices, shards(): lax.all_gather(up_weight, 'gy', axis=1, tiled=True)  129 us
    reduce_scatter x1, waiting for transfers between devices, shards(): lax.psum_scatter(up_partial.astype(jnp.bfloat16), 'gz', scatter_dimension...  119 us
    all_gather x1, waiting for transfers between devices, shards(): lax.all_gather(gate_weight, 'gy', axis=1, tiled=True)  117 us
    reduce_scatter x1, waiting for transfers between devices, shards(): lax.psum_scatter(gate_partial.astype(jnp.bfloat16), 'gz', scatter_dimensi...  116 us
    all_gather x1, waiting for transfers between devices, shards(): hidden = lax.all_gather(local_hidden, 'gz', axis=0, tiled=True)  100 us
    reduce_scatter x1, waiting for transfers between devices, shards(): lax.psum_scatter(down_partial.astype(jnp.bfloat16), 'gx', scatter_dimensi...  30.5 us
    dot_general x2, matrix products, column_product(): return jnp.dot(gathered, weight_piece, preferred_element_type=jnp.float32)  16.9 us
  transfers between devices with their start and end apart: 14, of which 11 were waited for; matrix products, arithmetic and copies ran while one was open for 3% of the time, Pallas kernels for 0%

profile of v1, /device:TPU:2, one launch (start us, length us, event | category | flops | bytes accessed | tf_op | source)
XLA Modules:
  0.0 809.7 jit_solution(5254276412785545997)
XLA Ops:
  6.5 0.7 all-gather.5.cloned.1.call-update
  7.3 0.7 all-gather.7.cloned.1.call-update
  8.1 2.9 collective-permute-start.1
  11.0 0.1 broadcast_in_dim.3
  11.1 0.9 constant_dynamic-update-slice_fusion.7
  12.1 1.8 collective-permute-done
  13.9 3.0 collective-permute-start.3
  16.9 2.6 collective-permute-done.2
  19.5 3.0 collective-permute-start.5
  22.5 2.6 collective-permute-done.4
  25.1 5.5 collective-permute-done.6
  30.7 117.3 %all-gather.5.cloned.1.call-done = bf16[1024,3584]{1,0:T(8,128)(2,1)} async-done(((bf16[1024,896]{1,0:T(8,128)(2,1)}), bf16[1024,3584]{1,0:T(8,128)(2,1)}) %all-gather.5.cloned.1.call-update) | async-done | bytes 7340048 | tf_op jit(solution)/shard_map/all_gather | solution.py:32
  148.0 8.5 %convolution_convert_fusion.1 = bf16[512,3584]{1,0:T(8,128)(2,1)} fusion(bf16[512,1024]{1,0:T(8,128)(2,1)S(1)} %constant_dynamic-update-slice_fusion, bf16[1024,3584]{1,0:T(8,128)(2,1)} %all-gather.5.cloned.1.call-done), kind=kOutput, calls=%fused_computation.1 | convolution fusion | flops 3759931392 | bytes 12058624 | tf_op jit(solution)/shard_map/dot_general | solution.py:30
  156.5 0.0 reduce-scatter.6.cloned.1.call-start
  156.6 128.8 %all-gather.7.cloned.1.call-done = bf16[1024,3584]{1,0:T(8,128)(2,1)} async-done(((bf16[1024,896]{1,0:T(8,128)(2,1)}), bf16[1024,3584]{1,0:T(8,128)(2,1)}) %all-gather.7.cloned.1.call-update) | async-done | bytes 7340048 | tf_op jit(solution)/shard_map/all_gather | solution.py:33
  285.4 8.4 %convolution_convert_fusion = bf16[512,3584]{1,0:T(8,128)(2,1)} fusion(bf16[512,1024]{1,0:T(8,128)(2,1)S(1)} %constant_dynamic-update-slice_fusion, bf16[1024,3584]{1,0:T(8,128)(2,1)} %all-gather.7.cloned.1.call-done), kind=kOutput, calls=%fused_computation | convolution fusion | flops 3759931392 | bytes 12058624 | tf_op jit(solution)/shard_map/dot_general | solution.py:30
  293.9 0.5 all-gather.11.cloned.1.call-update
  294.5 115.6 %reduce-scatter.4.cloned.1.call-done = bf16[64,3584]{1,0:T(8,128)(2,1)} async-done(((bf16[512,3584]{1,0:T(8,128)(2,1)}), bf16[64,3584]{1,0:T(8,128)(2,1)}) %reduce-scatter.4.cloned.1.call-update) | async-done | bytes 458768 | tf_op jit(solution)/shard_map/reduce_scatter | solution.py:35
  410.1 119.4 %reduce-scatter.6.cloned.1.call-done = bf16[64,3584]{1,0:T(8,128)(2,1)} async-done(((bf16[512,3584]{1,0:T(8,128)(2,1)}), bf16[64,3584]{1,0:T(8,128)(2,1)}) %reduce-scatter.6.cloned.1.call-update) | async-done | bytes 458768 | tf_op jit(solution)/shard_map/reduce_scatter | solution.py:38
  529.5 2.2 fusion.4
  531.8 131.0 %all-gather.11.cloned.1.call-done = bf16[3584,1024]{1,0:T(8,128)(2,1)} async-done(((bf16[896,1024]{1,0:T(8,128)(2,1)}), bf16[3584,1024]{1,0:T(8,128)(2,1)}) %all-gather.11.cloned.1.call-update) | async-done | bytes 7340048 | tf_op jit(solution)/shard_map/all_gather | solution.py:46
  662.8 100.5 %all-gather.9.cloned.1.call-done = bf16[512,3584]{1,0:T(8,128)(2,1)} async-done(((bf16[64,3584]{1,0:T(8,128)(2,1)}), bf16[512,3584]{1,0:T(8,128)(2,1)}) %all-gather.9.cloned.1.call-update) | async-done | bytes 3670032 | tf_op jit(solution)/shard_map/all_gather | solution.py:43
  763.3 9.1 %convolution_convert_fusion.2 = bf16[512,1024]{1,0:T(8,128)(2,1)} fusion(bf16[512,3584]{1,0:T(8,128)(2,1)} %all-gather.9.cloned.1.call-done, bf16[3584,1024]{1,0:T(8,128)(2,1)} %all-gather.11.cloned.1.call-done), kind=kOutput, calls=%fused_computation.2 | convolution fusion | flops 3758620672 | bytes 12058624 | tf_op jit(solution)/shard_map/dot_general | solution.py:44
  772.4 30.5 %reduce-scatter.8.cloned.1.call-done = bf16[64,1024]{1,0:T(8,128)(2,1)} async-done(((bf16[512,1024]{1,0:T(8,128)(2,1)}), bf16[64,1024]{1,0:T(8,128)(2,1)}) %reduce-scatter.8.cloned.1.call-update) | async-done | bytes 131088 | tf_op jit(solution)/shard_map/reduce_scatter | solution.py:49
  (24 shorter events, 0.4 us)
Async XLA Ops:
  6.5 141.5 %all-gather.5.cloned.1.call-start = ((), (), s32[]{:S(2)}) async-start(), calls=%async_computation.3 | async-start | bytes 9175040 | tf_op jit(solution)/shard_map/all_gather | solution.py:32
  7.3 278.1 %all-gather.7.cloned.1.call-start = ((), (), s32[]{:S(2)}) async-start(), calls=%async_computation.5 | async-start | bytes 9175040 | tf_op jit(solution)/shard_map/all_gather | solution.py:33
  8.0 402.1 %reduce-scatter.4.cloned.1.call-start = ((), (), s32[]{:S(2)}) async-start(), calls=%async_computation.4 | async-start | bytes 4128768 | tf_op jit(solution)/shard_map/reduce_scatter | solution.py:35
  8.1 5.8 collective-permute-start
  8.1 5.8 collective-permute-start.1
  13.9 5.6 collective-permute-start.2
  13.9 5.6 collective-permute-start.3
  19.5 5.6 collective-permute-start.4
  19.5 5.6 collective-permute-start.5
  25.1 5.6 collective-permute-start.6
  156.5 373.0 %reduce-scatter.6.cloned.1.call-start = ((), (), s32[]{:S(2)}) async-start(), calls=%async_computation.6 | async-start | bytes 4128768 | tf_op jit(solution)/shard_map/reduce_scatter | solution.py:38
  293.8 369.0 %all-gather.11.cloned.1.call-start = ((), (), s32[]{:S(2)}) async-start(), calls=%async_computation.8 | async-start | bytes 9175040 | tf_op jit(solution)/shard_map/all_gather | solution.py:46
  294.4 468.8 %all-gather.9.cloned.1.call-start = ((), (), s32[]{:S(2)}) async-start(), calls=%async_computation.7 | async-start | bytes 4128768 | tf_op jit(solution)/shard_map/all_gather | solution.py:43
  531.7 271.2 %reduce-scatter.8.cloned.1.call-start = ((), (), s32[]{:S(2)}) async-start(), calls=%async_computation.9 | async-start | bytes 1179648 | tf_op jit(solution)/shard_map/reduce_scatter | solution.py:49
Sparse Core Ops, SparseCore 0:
  9.2 138.7 all-gather.4
  149.8 135.5 all-gather.6
  289.6 120.4 reduce-scatter.3
  414.8 114.6 reduce-scatter.5
  531.1 131.6 all-gather.10
  665.3 97.9 all-gather.8
  772.5 30.3 reduce-scatter.7
